TPU v7x, 32 devices: a whole 2x2x4 slice. The times are simulated.
32 devices in a mesh: energy: 4 (over y, x), space: 8 (over z, core).
Axes of the slice: x: 2, y: 2, z: 4, core: 2. Of those that a mesh axis runs over, the one named last changes fastest.
Arguments:
- right_side: float32 [4, 64, 64, 512], P(None, 'space', None, 'energy')
- rate: float32 [64, 64, 512], P('space', None, 'energy'), may hold values from 0.5 to 2
- fields: float32 [2, 64, 64], P(None, 'space'), may hold values from -3 to 3
- speed: float32 [512], P('energy'), may hold values from 0.3 to 1
- regions: int32 [64, 64], P('space'), may hold values from 0 to 3
- contacts: int32 [64, 64], P('space'), may hold values 0 or 1
- offsets: int32 [4], replicated, may hold values from 12 to 24, as said below
- phonon: float32 [4, 2], replicated, may hold values from 0.1 to 0.6
Outputs:
- state: float32 [4, 64, 64, 512], P(None, 'space', None, 'energy')
- norms: float32 [2, 4], replicated
Inputs may be any that keep to these rules, and one draw needn't show every extreme that they name: `offsets`: each region's phonon energy lies between 12 and 24 bins; some region has exactly 24.
All inputs are finite; a program needn't handle non-finite values. No bound on the sum of `contacts` on one device may be relied on, other than what follows from the above.
Results may differ from a plain program's by a relative error of at most 0.0001.
Values sent between devices are 32-bit elements; how exact they have to be, the bound alone decides.
A program may use at most 64 MiB of HBM per device.

v0:
```python
import functools

import jax
import jax.numpy as jnp
from jax import lax
from jax.experimental import pallas as pl
from jax.experimental.pallas import tpu as pltpu
from jax.sharding import PartitionSpec as P

HOP = 24
REGIONS = 4
SWEEPS = 2
COEFS = 4
PAD = 8
ROWS = 16

diffusion = 0.25

MESH = pl.DeviceIdType.MESH


def kernel(
    n_energy,
    n_space,
    offsets_ref,
    phonon_ref,
    right_hbm,
    rate_hbm,
    fields_ref,
    speed_ref,
    regions_ref,
    contacts_ref,
    state_hbm,
    norms_ref,
    right,
    rate,
    field,
    cell_x,
    cell_y,
    cell_pin,
    cell_off,
    cell_absorb,
    cell_emit,
    inv_diag,
    inv_det,
    pack_low,
    pack_high,
    from_low,
    from_high,
    sums,
    in_sem,
    out_sem,
    x_send,
    x_recv,
    e_send,
    e_recv,
    n_send,
    n_recv,
):
    nx, ny, width = right.shape[1:]
    lanes_each = 1
    while lanes_each < HOP:
        lanes_each *= 2
    groups = width // lanes_each
    e = lax.axis_index("energy")
    s = lax.axis_index("space")
    total = n_energy * n_space
    me = e * n_space + s

    barrier = pltpu.get_barrier_semaphore()

    def greet(step, carry):
        other = lax.rem(me + step, total)
        pl.semaphore_signal(
            barrier,
            inc=1,
            device_id=(other // n_space, lax.rem(other, n_space)),
            device_id_type=MESH,
        )
        return carry

    lax.fori_loop(1, total, greet, 0)

    load_right = pltpu.make_async_copy(right_hbm, right, in_sem.at[0])
    load_rate = pltpu.make_async_copy(rate_hbm, rate, in_sem.at[1])
    load_right.start()
    load_rate.start()

    region = regions_ref[...]
    off = jnp.zeros_like(region)
    absorb = jnp.zeros(region.shape, jnp.float32)
    emit = jnp.zeros(region.shape, jnp.float32)
    for r in range(REGIONS):
        inside = region == r
        off = jnp.where(inside, offsets_ref[r], off)
        absorb = jnp.where(inside, phonon_ref[r, 0], absorb)
        emit = jnp.where(inside, phonon_ref[r, 1], emit)
    for source, target in (
        (fields_ref[0], cell_x),
        (fields_ref[1], cell_y),
        (contacts_ref[...], cell_pin),
        (off, cell_off),
        (absorb, cell_absorb),
        (emit, cell_emit),
    ):
        turned = source.T
        for x in range(nx):
            target[x] = jnp.broadcast_to(turned[:, x : x + 1], (ny, width))

    zero_rows = jnp.zeros((PAD, width), jnp.float32)
    for k in range(SWEEPS):
        for c in range(COEFS):
            for x in range(1, nx + 1):
                field[k, c, x, 0:PAD] = zero_rows
                field[k, c, x, PAD + ny : 2 * PAD + ny] = zero_rows

    zero_plane = jnp.zeros((ny, width), jnp.float32)

    @pl.when(s == 0)
    def _():
        for k in range(SWEEPS):
            for c in range(COEFS):
                field[k, c, 0, PAD : PAD + ny] = zero_plane

    @pl.when(s == n_space - 1)
    def _():
        for k in range(SWEEPS):
            for c in range(COEFS):
                field[k, c, nx + 1, PAD : PAD + ny] = zero_plane

    @pl.when(e == 0)
    def _():
        for k in range(SWEEPS):
            for q in range(from_low.shape[1]):
                from_low[k, q] = zero_plane

    @pl.when(e == n_energy - 1)
    def _():
        for k in range(SWEEPS):
            for q in range(from_high.shape[1]):
                from_high[k, q] = zero_plane

    load_rate.wait()
    load_right.wait()

    def solve(r, px, py, diag, inv_d, inv_t):
        first = (diag * r[0] - px * r[1] - py * r[2]) * inv_t
        return (
            first,
            (r[1] + px * first) * inv_d,
            (r[2] + py * first) * inv_d,
            r[3] * inv_d,
        )

    def first_state(x, carry):
        for y in range(0, ny, ROWS):
            rows = pl.ds(y, ROWS)
            diag = rate[x, rows] + 4.0 * diffusion
            px, py = cell_x[x, rows], cell_y[x, rows]
            inv_d = 1.0 / diag
            inv_t = 1.0 / (diag * diag + px * px + py * py)
            inv_diag[x, rows] = inv_d
            inv_det[x, rows] = inv_t
            r = [right[c, x, rows] for c in range(COEFS)]
            u = solve(r, px, py, diag, inv_d, inv_t)
            pinned = cell_pin[x, rows] == 1
            for c in range(COEFS):
                field[0, c, x + 1, pl.ds(PAD + y, ROWS)] = jnp.where(pinned, r[c], u[c])
        return carry

    lax.fori_loop(0, nx, first_state, 0)
    pl.semaphore_wait(barrier, total - 1)

    plane_group = lax.broadcasted_iota(jnp.int32, (ny, width), 1) // lanes_each
    inner = pl.ds(PAD, ny)

    def to_right(k):
        return pltpu.make_async_remote_copy(
            src_ref=field.at[k, :, nx, inner],
            dst_ref=field.at[k, :, 0, inner],
            send_sem=x_send.at[k, 0],
            recv_sem=x_recv.at[k, 0],
            device_id=(e, s + 1),
            device_id_type=MESH,
        )

    def to_left(k):
        return pltpu.make_async_remote_copy(
            src_ref=field.at[k, :, 1, inner],
            dst_ref=field.at[k, :, nx + 1, inner],
            send_sem=x_send.at[k, 1],
            recv_sem=x_recv.at[k, 1],
            device_id=(e, s - 1),
            device_id_type=MESH,
        )

    def to_upper(k):
        return pltpu.make_async_remote_copy(
            src_ref=pack_high.at[k],
            dst_ref=from_low.at[k],
            send_sem=e_send.at[k, 0],
            recv_sem=e_recv.at[k, 0],
            device_id=(e + 1, s),
            device_id_type=MESH,
        )

    def to_lower(k):
        return pltpu.make_async_remote_copy(
            src_ref=pack_low.at[k],
            dst_ref=from_high.at[k],
            send_sem=e_send.at[k, 1],
            recv_sem=e_recv.at[k, 1],
            device_id=(e - 1, s),
            device_id_type=MESH,
        )

    has_right, has_left = s < n_space - 1, s > 0
    has_upper, has_lower = e < n_energy - 1, e > 0

    def exchange(k):
        @pl.when(has_right)
        def _():
            to_right(k).start()

        @pl.when(has_left)
        def _():
            to_left(k).start()

        for q in range(pack_low.shape[1]):
            low = zero_plane
            high = zero_plane
            for j in range(groups):
                x = q * groups + j
                if x >= nx:
                    break
                plane = field[k, 0, x + 1, inner]
                here = plane_group == j
                turn_low = lanes_each * j
                turn_high = (lanes_each * (j + 1)) % width
                rolled_low = pltpu.roll(plane, turn_low, 1) if turn_low else plane
                rolled_high = pltpu.roll(plane, turn_high, 1) if turn_high else plane
                low = jnp.where(here, rolled_low, low)
                high = jnp.where(here, rolled_high, high)
            pack_low[k, q] = low
            pack_high[k, q] = high

        @pl.when(has_upper)
        def _():
            to_upper(k).start()

        @pl.when(has_lower)
        def _():
            to_lower(k).start()

    def arrive(k):
        @pl.when(has_lower)
        def _():
            to_upper(k).wait_recv()

        @pl.when(has_upper)
        def _():
            to_lower(k).wait_recv()

        @pl.when(has_left)
        def _():
            to_right(k).wait_recv()

        @pl.when(has_right)
        def _():
            to_left(k).wait_recv()

    lane = lax.broadcasted_iota(jnp.int32, (ROWS, width), 1)
    velocity = jnp.broadcast_to(0.5 * speed_ref[...], (ROWS, width))

    def residual(k, x, y, j, q):
        rows = pl.ds(y, ROWS)
        mid = pl.ds(PAD + y, ROWS)
        f = [field[k, c, x + 1, mid] for c in range(COEFS)]
        xp = [field[k, c, x + 2, mid] for c in range(COEFS)]
        xm = [field[k, c, x, mid] for c in range(COEFS)]
        yp = [field[k, c, x + 1, pl.ds(PAD + y + 1, ROWS)] for c in range(COEFS)]
        ym = [field[k, c, x + 1, pl.ds(PAD + y - 1, ROWS)] for c in range(COEFS)]
        diag = rate[x, rows] + 4.0 * diffusion
        px, py = cell_x[x, rows], cell_y[x, rows]
        nb = [xp[c] + xm[c] + (yp[c] + ym[c]) for c in range(COEFS)]
        back_low = (lanes_each * (groups - 1 - j)) % width
        back_high = (width - lanes_each * j) % width
        low = from_low[k, q, rows]
        high = from_high[k, q, rows]
        low = pltpu.roll(low, back_low, 1) if back_low else low
        high = pltpu.roll(high, back_high, 1) if back_high else high
        beyond = jnp.where(lane < width // 2, high, low)
        off = cell_off[x, rows]
        below = jnp.take_along_axis(
            jnp.where(lane < width - off, f[0], beyond),
            lax.rem(lane - off + width, width),
            axis=1,
            mode="promise_in_bounds",
        )
        above = jnp.take_along_axis(
            jnp.where(lane < off, beyond, f[0]),
            lax.rem(lane + off, width),
            axis=1,
            mode="promise_in_bounds",
        )
        scatter = cell_absorb[x, rows] * below + cell_emit[x, rows] * above
        image = [
            diag * f[0]
            + px * f[1]
            + py * f[2]
            - diffusion * nb[0]
            + velocity * (xp[1] - xm[1] + (yp[2] - ym[2]))
            - scatter,
            diag * f[1] - px * f[0] - diffusion * nb[1] + velocity * (xp[0] - xm[0]),
            diag * f[2] - py * f[0] - diffusion * nb[2] + velocity * (yp[0] - ym[0]),
            diag * f[3] - diffusion * nb[3],
        ]
        pinned = cell_pin[x, rows] == 1
        resid = [
            right[c, x, rows] - jnp.where(pinned, f[c], image[c]) for c in range(COEFS)
        ]
        return f, resid, pinned, px, py, diag

    def folded(value):
        square = value * value
        out = square[0:8]
        for i in range(8, ROWS, 8):
            out = out + square[i : i + 8]
        return out

    def sweep(k, last):
        def planes(q, carry):
            acc = list(carry)
            for j in range(groups):
                x = q * groups + j
                for y in range(0, ny, ROWS):
                    f, resid, pinned, px, py, diag = residual(k, x, y, j, q)
                    for c in range(COEFS):
                        acc[c] = acc[c] + folded(resid[c])
                    if not last:
                        rows = pl.ds(y, ROWS)
                        u = solve(resid, px, py, diag, inv_diag[x, rows], inv_det[x, rows])
                        for c in range(COEFS):
                            field[k + 1, c, x + 1, pl.ds(PAD + y, ROWS)] = f[c] + jnp.where(
                                pinned, resid[c], u[c]
                            )
            return tuple(acc)

        start = tuple(jnp.zeros((8, width), jnp.float32) for _ in range(COEFS))
        return lax.fori_loop(0, nx // groups, planes, start)

    partial = []
    store = pltpu.make_async_copy(
        field.at[SWEEPS - 1, :, pl.ds(1, nx), inner], state_hbm, out_sem
    )
    for k in range(SWEEPS):
        exchange(k)
        if k == SWEEPS - 1:
            store.start()
        arrive(k)
        partial.extend(sweep(k, k == SWEEPS - 1))

    spot = lax.broadcasted_iota(jnp.int32, (1, width), 1)
    mine = jnp.zeros((1, width), jnp.float32)
    for i, value in enumerate(partial):
        whole = jnp.sum(jnp.sum(value, axis=0, keepdims=True), axis=1, keepdims=True)
        mine = jnp.where(spot == i, whole, mine)
    sums[me] = mine

    def tell(step):
        other = lax.rem(me + step, total)
        return pltpu.make_async_remote_copy(
            src_ref=sums.at[me],
            dst_ref=sums.at[me],
            send_sem=n_send.at[other],
            recv_sem=n_recv.at[me],
            device_id=(other // n_space, lax.rem(other, n_space)),
            device_id_type=MESH,
        )

    def heard(step):
        other = lax.rem(me + step, total)
        return pltpu.make_async_remote_copy(
            src_ref=sums.at[other],
            dst_ref=sums.at[other],
            send_sem=n_send.at[other],
            recv_sem=n_recv.at[other],
            device_id=(other // n_space, lax.rem(other, n_space)),
            device_id_type=MESH,
        )

    def tell_start(step, carry):
        tell(step).start()
        return carry

    lax.fori_loop(1, total, tell_start, 0)
    for k in range(SWEEPS):

        @pl.when(has_right)
        def _():
            to_right(k).wait_send()

        @pl.when(has_left)
        def _():
            to_left(k).wait_send()

        @pl.when(has_upper)
        def _():
            to_upper(k).wait_send()

        @pl.when(has_lower)
        def _():
            to_lower(k).wait_send()

    store.wait()

    def heard_wait(step, carry):
        heard(step).wait_recv()
        return carry

    lax.fori_loop(1, total, heard_wait, 0)

    def tell_wait(step, carry):
        tell(step).wait_send()
        return carry

    lax.fori_loop(1, total, tell_wait, 0)
    norm = jnp.sqrt(jnp.sum(sums[...], axis=0))
    norm = jnp.broadcast_to(norm, (8, width))
    for k in range(SWEEPS):
        turned = pltpu.roll(norm, width - COEFS * k, 1) if k else norm
        norms_ref[k : k + 1, :] = turned[0:1, 0:COEFS]


def solution(mesh):
    n_energy, n_space = mesh.shape["energy"], mesh.shape["space"]

    def local(right_side, rate, fields, speed, regions, contacts, offsets, phonon):
        coefs, nx, ny, width = right_side.shape
        lanes_each = 1
        while lanes_each < HOP:
            lanes_each *= 2
        packs = -(-nx // (width // lanes_each))
        plane = (nx, ny, width)
        vmem = pl.BlockSpec(memory_space=pltpu.VMEM)
        smem = pl.BlockSpec(memory_space=pltpu.SMEM)
        hbm = pl.BlockSpec(memory_space=pl.ANY)
        f32 = jnp.float32
        pack = pltpu.VMEM((SWEEPS, packs, ny, width), f32)
        return pl.pallas_call(
            functools.partial(kernel, n_energy, n_space),
            out_shape=(
                jax.ShapeDtypeStruct(right_side.shape, f32),
                jax.ShapeDtypeStruct((SWEEPS, coefs), f32),
            ),
            in_specs=[smem, smem, hbm, hbm, vmem, vmem, vmem, vmem],
            out_specs=(hbm, vmem),
            scratch_shapes=[
                pltpu.VMEM(right_side.shape, f32),
                pltpu.VMEM(plane, f32),
                pltpu.VMEM((SWEEPS, coefs, nx + 2, ny + 2 * PAD, width), f32),
                pltpu.VMEM(plane, f32),
                pltpu.VMEM(plane, f32),
                pltpu.VMEM(plane, jnp.int32),
                pltpu.VMEM(plane, jnp.int32),
                pltpu.VMEM(plane, f32),
                pltpu.VMEM(plane, f32),
                pltpu.VMEM(plane, f32),
                pltpu.VMEM(plane, f32),
                pack,
                pack,
                pack,
                pack,
                pltpu.VMEM((n_energy * n_space, 1, width), f32),
                pltpu.SemaphoreType.DMA((2,)),
                pltpu.SemaphoreType.DMA,
                pltpu.SemaphoreType.DMA((SWEEPS, 2)),
                pltpu.SemaphoreType.DMA((SWEEPS, 2)),
                pltpu.SemaphoreType.DMA((SWEEPS, 2)),
                pltpu.SemaphoreType.DMA((SWEEPS, 2)),
                pltpu.SemaphoreType.DMA((n_energy * n_space,)),
                pltpu.SemaphoreType.DMA((n_energy * n_space,)),
            ],
            compiler_params=pltpu.CompilerParams(collective_id=0, has_side_effects=True),
        )(offsets, phonon, right_side, rate, fields, speed.reshape(1, width), regions, contacts)

    in_specs = (
        P(None, "space", None, "energy"),
        P("space", None, "energy"),
        P(None, "space", None),
        P("energy"),
        P("space", None),
        P("space", None),
        P(),
        P(),
    )
    out_specs = (P(None, "space", None, "energy"), P())
    return jax.shard_map(local, mesh=mesh, in_specs=in_specs, out_specs=out_specs, check_vma=False)
```

profile of v0, /device:TPU:0, one launch (start us, length us, event | category | flops | bytes accessed | tf_op | source)
XLA Modules:
  0.0 29.1 jit_solution(17466350527482795021)
XLA Ops:
  0.6 0.0 copy-start
  0.6 0.7 %copy-done = f32[4,2]{0,1:T(2,128)S(1)} copy-done((f32[4,2]{0,1:T(2,128)S(1)}, f32[4,2]{0,1:T(2,128)}, u32[]{:S(2)}) %copy-start) | copy-done | bytes 56
  1.3 0.7 %copy.10.phonon_ref = f32[4,2]{1,0:T(4,128)} copy(f32[4,2]{0,1:T(2,128)S(1)} %copy-done) | data formatting | bytes 64 | tf_op args[7]
  2.0 24.2 %shard_map.95 = (f32[4,8,64,128]{3,2,1,0:T(8,128)}, f32[2,4]{1,0:T(2,128)}) custom-call(s32[4]{0:T(128)} %offsets_ref.1, f32[4,2]{1,0:T(4,128)} %copy.10.phonon_ref, f32[4,8,64,128]{3,2,1,0:T(8,128)} %right_hbm.1, f32[8,64,128]{2,1,0:T(8,128)} %rate_hbm.1, f32[2,8,64]{2,1,0:T(8,128)} %fields_ref.1, f32[1,128]{1,0:T(1,128)} %bitcast.1, s32[8,64]{1,0:T(8,128)} %regions_ref.1, ...), custom_call_target="tpu_custom_call" | custom-call | tf_op jit(solution)/shard_map/pallas_call | solution.py:450
  26.2 0.0 copy-start.1
  26.2 2.3 %copy.13 = f32[4,8,64,128]{3,2,1,0:T(8,128)} copy(f32[4,8,64,128]{3,2,1,0:T(8,128)} %get-tuple-element.4) | data formatting | bytes 2097152
  28.5 0.0 copy-done.1
  28.5 0.6 %copy.14 = f32[2,4]{1,0:T(2,128)} copy(f32[2,4]{1,0:T(2,128)S(1)} %copy-done.1) | data formatting | bytes 64
Async XLA Ops:
  0.6 0.7 %copy-start = (f32[4,2]{0,1:T(2,128)S(1)}, f32[4,2]{0,1:T(2,128)}, u32[]{:S(2)}) copy-start(f32[4,2]{0,1:T(2,128)} %param.15) | copy-start | bytes 100
  26.2 2.3 %copy-start.1 = (f32[2,4]{1,0:T(2,128)S(1)}, f32[2,4]{1,0:T(2,128)}, u32[]{:S(2)}) copy-start(f32[2,4]{1,0:T(2,128)} %get-tuple-element.5) | copy-start | bytes 100
where the time goes:
time: 29.3 us; the launch traced here: 29.1 us
  Pallas kernels  24.2 us (83%)
  local copies, waits for them, and re-layouts  4.21 us (14%)
  between operations  0.66 us (2%)
    pallas_call x1, Pallas kernels, local(): pl.pallas_call(functools.partial(kernel, n_energy, n_space), out_shape=(j...  24.2 us
    unnamed x7, local copies, waits for them, and re-layouts  4.21 us

commit v1 on v0

v1 whole, which is shorter than its diff:
```python
import functools

import jax
import jax.numpy as jnp
from jax import lax
from jax.experimental import pallas as pl
from jax.experimental.pallas import tpu as pltpu
from jax.sharding import PartitionSpec as P

HOP = 24
REGIONS = 4
SWEEPS = 2
COEFS = 4
PAD = 8
ROWS = 16

diffusion = 0.25

MESH = pl.DeviceIdType.MESH


def kernel(
    n_energy,
    n_space,
    offsets_hbm,
    phonon_hbm,
    right_hbm,
    rate_hbm,
    fields_hbm,
    speed_hbm,
    regions_hbm,
    contacts_hbm,
    state_ref,
    sums_ref,
    offsets_ref,
    phonon_ref,
    fields_ref,
    speed_ref,
    regions_ref,
    contacts_ref,
    right,
    rate,
    field,
    cell_x,
    cell_y,
    cell_pin,
    cell_off,
    cell_absorb,
    cell_emit,
    inv_diag,
    inv_det,
    pack_low,
    pack_high,
    from_low,
    from_high,
    beyond,
    along_energy,
    along_space,
    in_sem,
    out_sem,
    x_send,
    x_recv,
    e_send,
    e_recv,
    n_send,
    n_recv,
    m_send,
    m_recv,
):
    nx, ny, width = right.shape[1:]
    groups = width // HOP
    e = lax.axis_index("energy")
    s = lax.axis_index("space")

    barrier = pltpu.get_barrier_semaphore()
    for step in range(1, n_energy):
        pl.semaphore_signal(
            barrier,
            inc=1,
            device_id=(lax.rem(e + step, n_energy), s),
            device_id_type=MESH,
        )
    for step in range(1, n_space):
        pl.semaphore_signal(
            barrier,
            inc=1,
            device_id=(e, lax.rem(s + step, n_space)),
            device_id_type=MESH,
        )

    loads = [
        pltpu.make_async_copy(source, target, in_sem.at[i])
        for i, (source, target) in enumerate(
            (
                (offsets_hbm, offsets_ref),
                (phonon_hbm, phonon_ref),
                (fields_hbm, fields_ref),
                (speed_hbm, speed_ref),
                (regions_hbm, regions_ref),
                (contacts_hbm, contacts_ref),
                (rate_hbm, rate),
                (right_hbm, right),
            )
        )
    ]
    for load in loads:
        load.start()

    zero_rows = jnp.zeros((PAD, width), jnp.float32)
    for k in range(SWEEPS):
        for c in range(COEFS):
            for x in range(1, nx + 1):
                field[k, c, x, 0:PAD] = zero_rows
                field[k, c, x, PAD + ny : 2 * PAD + ny] = zero_rows

    zero_plane = jnp.zeros((ny, width), jnp.float32)

    @pl.when(s == 0)
    def _():
        for k in range(SWEEPS):
            for c in range(COEFS):
                field[k, c, 0, PAD : PAD + ny] = zero_plane

    @pl.when(s == n_space - 1)
    def _():
        for k in range(SWEEPS):
            for c in range(COEFS):
                field[k, c, nx + 1, PAD : PAD + ny] = zero_plane

    @pl.when(e == 0)
    def _():
        for k in range(SWEEPS):
            from_low[k] = jnp.zeros(from_low.shape[1:], jnp.float32)

    @pl.when(e == n_energy - 1)
    def _():
        for k in range(SWEEPS):
            from_high[k] = jnp.zeros(from_high.shape[1:], jnp.float32)

    for load in loads[:-2]:
        load.wait()

    region = regions_ref[...]
    off = jnp.zeros_like(region)
    absorb = jnp.zeros(region.shape, jnp.float32)
    emit = jnp.zeros(region.shape, jnp.float32)
    for r in range(REGIONS):
        inside = region == r
        off = jnp.where(inside, offsets_ref[r], off)
        absorb = jnp.where(inside, phonon_ref[0, r], absorb)
        emit = jnp.where(inside, phonon_ref[1, r], emit)
    for source, target in (
        (fields_ref[0], cell_x),
        (fields_ref[1], cell_y),
        (contacts_ref[...], cell_pin),
        (off, cell_off),
        (absorb, cell_absorb),
        (emit, cell_emit),
    ):
        turned = source.T
        for x in range(nx):
            target[x] = jnp.broadcast_to(turned[:, x : x + 1], (ny, width))

    for load in loads[-2:]:
        load.wait()

    def solve(r, px, py, diag, inv_d, inv_t):
        first = (diag * r[0] - px * r[1] - py * r[2]) * inv_t
        return (
            first,
            (r[1] + px * first) * inv_d,
            (r[2] + py * first) * inv_d,
            r[3] * inv_d,
        )

    def first_state(x, carry):
        for y in range(0, ny, ROWS):
            rows = pl.ds(y, ROWS)
            diag = rate[x, rows] + 4.0 * diffusion
            px, py = cell_x[x, rows], cell_y[x, rows]
            inv_d = 1.0 / diag
            inv_t = 1.0 / (diag * diag + px * px + py * py)
            inv_diag[x, rows] = inv_d
            inv_det[x, rows] = inv_t
            r = [right[c, x, rows] for c in range(COEFS)]
            u = solve(r, px, py, diag, inv_d, inv_t)
            pinned = cell_pin[x, rows] == 1
            for c in range(COEFS):
                field[0, c, x + 1, pl.ds(PAD + y, ROWS)] = jnp.where(pinned, r[c], u[c])
        return carry

    lax.fori_loop(0, nx, first_state, 0)
    pl.semaphore_wait(barrier, n_energy + n_space - 2)

    unit_lane = lax.broadcasted_iota(jnp.int32, (8, width), 1)
    units = [(x, y) for x in range(nx) for y in range(0, ny, 8)]
    inner = pl.ds(PAD, ny)

    def to_right(k):
        return pltpu.make_async_remote_copy(
            src_ref=field.at[k, :, nx, inner],
            dst_ref=field.at[k, :, 0, inner],
            send_sem=x_send.at[k, 0],
            recv_sem=x_recv.at[k, 0],
            device_id=(e, s + 1),
            device_id_type=MESH,
        )

    def to_left(k):
        return pltpu.make_async_remote_copy(
            src_ref=field.at[k, :, 1, inner],
            dst_ref=field.at[k, :, nx + 1, inner],
            send_sem=x_send.at[k, 1],
            recv_sem=x_recv.at[k, 1],
            device_id=(e, s - 1),
            device_id_type=MESH,
        )

    def to_upper(k):
        return pltpu.make_async_remote_copy(
            src_ref=pack_high.at[k],
            dst_ref=from_low.at[k],
            send_sem=e_send.at[k, 0],
            recv_sem=e_recv.at[k, 0],
            device_id=(e + 1, s),
            device_id_type=MESH,
        )

    def to_lower(k):
        return pltpu.make_async_remote_copy(
            src_ref=pack_low.at[k],
            dst_ref=from_high.at[k],
            send_sem=e_send.at[k, 1],
            recv_sem=e_recv.at[k, 1],
            device_id=(e - 1, s),
            device_id_type=MESH,
        )

    has_right, has_left = s < n_space - 1, s > 0
    has_upper, has_lower = e < n_energy - 1, e > 0

    def turn(value, by):
        by = by % width
        return pltpu.roll(value, by, 1) if by else value

    def exchange(k):
        @pl.when(has_right)
        def _():
            to_right(k).start()

        @pl.when(has_left)
        def _():
            to_left(k).start()

        for q in range(pack_low.shape[1]):
            low = jnp.zeros((8, width), jnp.float32)
            high = jnp.zeros((8, width), jnp.float32)
            for j, (x, y) in enumerate(units[q * groups : (q + 1) * groups]):
                part = field[k, 0, x + 1, pl.ds(PAD + y, 8)]
                here = (unit_lane >= HOP * j) & (unit_lane < HOP * (j + 1))
                low = jnp.where(here, turn(part, HOP * j), low)
                high = jnp.where(here, turn(part, HOP * (j + 1)), high)
            pack_low[k, q] = low
            pack_high[k, q] = high

        @pl.when(has_upper)
        def _():
            to_upper(k).start()

        @pl.when(has_lower)
        def _():
            to_lower(k).start()

    def arrive(k):
        @pl.when(has_lower)
        def _():
            to_upper(k).wait_recv()

        @pl.when(has_upper)
        def _():
            to_lower(k).wait_recv()

        @pl.when(has_left)
        def _():
            to_right(k).wait_recv()

        @pl.when(has_right)
        def _():
            to_left(k).wait_recv()

        for i, (x, y) in enumerate(units):
            q, j = i // groups, i % groups
            beyond[x, pl.ds(y, 8)] = jnp.where(
                unit_lane < width // 2,
                turn(from_high[k, q], -HOP * j),
                turn(from_low[k, q], -HOP * (j + 1)),
            )

    lane = lax.broadcasted_iota(jnp.int32, (ROWS, width), 1)
    velocity = jnp.broadcast_to(0.5 * speed_ref[...], (ROWS, width))

    def residual(k, x, y):
        rows = pl.ds(y, ROWS)
        mid = pl.ds(PAD + y, ROWS)
        f = [field[k, c, x + 1, mid] for c in range(COEFS)]
        xp = [field[k, c, x + 2, mid] for c in range(COEFS)]
        xm = [field[k, c, x, mid] for c in range(COEFS)]
        yp = [field[k, c, x + 1, pl.ds(PAD + y + 1, ROWS)] for c in range(COEFS)]
        ym = [field[k, c, x + 1, pl.ds(PAD + y - 1, ROWS)] for c in range(COEFS)]
        diag = rate[x, rows] + 4.0 * diffusion
        px, py = cell_x[x, rows], cell_y[x, rows]
        nb = [xp[c] + xm[c] + (yp[c] + ym[c]) for c in range(COEFS)]
        outside = beyond[x, rows]
        off = cell_off[x, rows]
        below = jnp.take_along_axis(
            jnp.where(lane < width - off, f[0], outside),
            lax.rem(lane - off + width, width),
            axis=1,
            mode="promise_in_bounds",
        )
        above = jnp.take_along_axis(
            jnp.where(lane < off, outside, f[0]),
            lax.rem(lane + off, width),
            axis=1,
            mode="promise_in_bounds",
        )
        scatter = cell_absorb[x, rows] * below + cell_emit[x, rows] * above
        image = [
            diag * f[0]
            + px * f[1]
            + py * f[2]
            - diffusion * nb[0]
            + velocity * (xp[1] - xm[1] + (yp[2] - ym[2]))
            - scatter,
            diag * f[1] - px * f[0] - diffusion * nb[1] + velocity * (xp[0] - xm[0]),
            diag * f[2] - py * f[0] - diffusion * nb[2] + velocity * (yp[0] - ym[0]),
            diag * f[3] - diffusion * nb[3],
        ]
        pinned = cell_pin[x, rows] == 1
        resid = [
            right[c, x, rows] - jnp.where(pinned, f[c], image[c]) for c in range(COEFS)
        ]
        return f, resid, pinned, px, py, diag

    def folded(value):
        square = value * value
        out = square[0:8]
        for i in range(8, ROWS, 8):
            out = out + square[i : i + 8]
        return out

    def sweep(k, last):
        def plane(x, carry):
            acc = list(carry)
            for y in range(0, ny, ROWS):
                f, resid, pinned, px, py, diag = residual(k, x, y)
                for c in range(COEFS):
                    acc[c] = acc[c] + folded(resid[c])
                if not last:
                    rows = pl.ds(y, ROWS)
                    u = solve(resid, px, py, diag, inv_diag[x, rows], inv_det[x, rows])
                    for c in range(COEFS):
                        field[k + 1, c, x + 1, pl.ds(PAD + y, ROWS)] = f[c] + jnp.where(
                            pinned, resid[c], u[c]
                        )
            return tuple(acc)

        start = tuple(jnp.zeros((8, width), jnp.float32) for _ in range(COEFS))
        return lax.fori_loop(0, nx, plane, start)

    partial = []
    store = pltpu.make_async_copy(
        field.at[SWEEPS - 1, :, pl.ds(1, nx), inner], state_ref, out_sem
    )
    for k in range(SWEEPS):
        exchange(k)
        if k == SWEEPS - 1:
            store.start()
        arrive(k)
        partial.extend(sweep(k, k == SWEEPS - 1))

    spot = lax.broadcasted_iota(jnp.int32, (1, width), 1)
    mine = jnp.zeros((1, width), jnp.float32)
    for i, value in enumerate(partial):
        whole = jnp.sum(jnp.sum(value, axis=0, keepdims=True), axis=1, keepdims=True)
        mine = jnp.where(spot == i, whole, mine)
    along_energy[e] = mine

    def tell(sums, size, place, to, sems, step):
        return pltpu.make_async_remote_copy(
            src_ref=sums.at[place],
            dst_ref=sums.at[place],
            send_sem=sems[0].at[step],
            recv_sem=sems[1].at[place],
            device_id=to(lax.rem(place + step, size)),
            device_id_type=MESH,
        )

    def heard(sums, size, place, to, sems, step):
        other = lax.rem(place + step, size)
        return pltpu.make_async_remote_copy(
            src_ref=sums.at[other],
            dst_ref=sums.at[other],
            send_sem=sems[0].at[step],
            recv_sem=sems[1].at[other],
            device_id=to(other),
            device_id_type=MESH,
        )

    first = (along_energy, n_energy, e, lambda i: (i, s), (n_send, n_recv))
    second = (along_space, n_space, s, lambda i: (e, i), (m_send, m_recv))
    for step in range(1, n_energy):
        tell(*first, step).start()
    for step in range(1, n_energy):
        heard(*first, step).wait_recv()
    along_space[s] = jnp.sum(along_energy[...], axis=0)
    for step in range(1, n_space):
        tell(*second, step).start()
    for k in range(SWEEPS):

        @pl.when(has_right)
        def _():
            to_right(k).wait_send()

        @pl.when(has_left)
        def _():
            to_left(k).wait_send()

        @pl.when(has_upper)
        def _():
            to_upper(k).wait_send()

        @pl.when(has_lower)
        def _():
            to_lower(k).wait_send()

    for step in range(1, n_energy):
        tell(*first, step).wait_send()
    store.wait()
    for step in range(1, n_space):
        heard(*second, step).wait_recv()
    for step in range(1, n_space):
        tell(*second, step).wait_send()
    sums_ref[...] = jnp.sum(along_space[...], axis=0)


def finish(state, sums_ref, state_hbm, norms_ref, sem):
    store = pltpu.make_async_copy(state, state_hbm, sem)
    store.start()
    width = sums_ref.shape[1]
    norm = jnp.broadcast_to(jnp.sqrt(sums_ref[...]), (8, width))
    for k in range(SWEEPS):
        turned = pltpu.roll(norm, width - COEFS * k, 1) if k else norm
        norms_ref[k : k + 1, :] = turned[0:1, 0:COEFS]
    store.wait()


def solution(mesh):
    n_energy, n_space = mesh.shape["energy"], mesh.shape["space"]

    def local(right_side, rate, fields, speed, regions, contacts, offsets, phonon):
        coefs, nx, ny, width = right_side.shape
        packs = -(-(nx * ny // 8) // (width // HOP))
        plane = (nx, ny, width)
        vmem = pl.BlockSpec(memory_space=pltpu.VMEM)
        hbm = pl.BlockSpec(memory_space=pl.ANY)
        f32 = jnp.float32
        pack = pltpu.VMEM((SWEEPS, packs, 8, width), f32)
        state, sums = pl.pallas_call(
            functools.partial(kernel, n_energy, n_space),
            out_shape=(
                pltpu.VMEM(right_side.shape, f32),
                pltpu.VMEM((1, width), f32),
            ),
            in_specs=[pl.BlockSpec(memory_space=pltpu.HBM)] * 8,
            out_specs=(vmem, vmem),
            scratch_shapes=[
                pltpu.SMEM(offsets.shape, offsets.dtype),
                pltpu.SMEM((phonon.shape[1], phonon.shape[0]), f32),
                pltpu.VMEM(fields.shape, f32),
                pltpu.VMEM((1, width), f32),
                pltpu.VMEM(regions.shape, regions.dtype),
                pltpu.VMEM(contacts.shape, contacts.dtype),
                pltpu.VMEM(right_side.shape, f32),
                pltpu.VMEM(plane, f32),
                pltpu.VMEM((SWEEPS, coefs, nx + 2, ny + 2 * PAD, width), f32),
                pltpu.VMEM(plane, f32),
                pltpu.VMEM(plane, f32),
                pltpu.VMEM(plane, jnp.int32),
                pltpu.VMEM(plane, jnp.int32),
                pltpu.VMEM(plane, f32),
                pltpu.VMEM(plane, f32),
                pltpu.VMEM(plane, f32),
                pltpu.VMEM(plane, f32),
                pack,
                pack,
                pack,
                pack,
                pltpu.VMEM(plane, f32),
                pltpu.VMEM((n_energy, 1, width), f32),
                pltpu.VMEM((n_space, 1, width), f32),
                pltpu.SemaphoreType.DMA((8,)),
                pltpu.SemaphoreType.DMA,
                pltpu.SemaphoreType.DMA((SWEEPS, 2)),
                pltpu.SemaphoreType.DMA((SWEEPS, 2)),
                pltpu.SemaphoreType.DMA((SWEEPS, 2)),
                pltpu.SemaphoreType.DMA((SWEEPS, 2)),
                pltpu.SemaphoreType.DMA((n_energy,)),
                pltpu.SemaphoreType.DMA((n_energy,)),
                pltpu.SemaphoreType.DMA((n_space,)),
                pltpu.SemaphoreType.DMA((n_space,)),
            ],
            compiler_params=pltpu.CompilerParams(
                collective_id=0, has_side_effects=True, vmem_limit_bytes=24 << 20
            ),
        )(
            *(
                pltpu.with_memory_space_constraint(value, pltpu.HBM)
                for value in (
                    offsets,
                    phonon.T,
                    right_side,
                    rate,
                    fields,
                    speed.reshape(1, width),
                    regions,
                    contacts,
                )
            )
        )
        return pl.pallas_call(
            finish,
            out_shape=(
                jax.ShapeDtypeStruct(right_side.shape, f32),
                jax.ShapeDtypeStruct((SWEEPS, coefs), f32),
            ),
            in_specs=[vmem, vmem],
            out_specs=(hbm, vmem),
            scratch_shapes=[pltpu.SemaphoreType.DMA],
            compiler_params=pltpu.CompilerParams(vmem_limit_bytes=8 << 20),
        )(state, sums)

    in_specs = (
        P(None, "space", None, "energy"),
        P("space", None, "energy"),
        P(None, "space", None),
        P("energy"),
        P("space", None),
        P("space", None),
        P(),
        P(),
    )
    out_specs = (P(None, "space", None, "energy"), P())
    return jax.shard_map(local, mesh=mesh, in_specs=in_specs, out_specs=out_specs, check_vma=False)
```

time: 29.3 us -> 25.4 us (0.87)
  local copies, waits for them, and re-layouts: 4.21 us -> 0 us
  Pallas kernels: 24.2 us -> 24.6 us
    unnamed x7 -> x0, local copies, waits for them, and re-layouts: 4.21 us -> none
    pallas_call x1 -> x2, Pallas kernels: 24.2 us -> 24.6 us  [the longest x1 23 us: local(): pl.pallas_call(functools.partial(kernel, n_energy, n_space), out_shape=(p...]
where the time goes in v1:
time: 25.4 us; the launch traced here: 25.2 us
  Pallas kernels  24.6 us (97%)
  between operations  0.64 us (3%)
    pallas_call x1, Pallas kernels, local(): pl.pallas_call(functools.partial(kernel, n_energy, n_space), out_shape=(p...  23 us
    pallas_call x1, Pallas kernels, local(): pl.pallas_call(finish, out_shape=(jax.ShapeDtypeStruct(right_side.shape,...  1.54 us

profile of v1, /device:TPU:0, one launch (start us, length us, event | category | flops | bytes accessed | tf_op | source)
XLA Modules:
  0.0 25.2 jit_solution(17990134139970251249)
XLA Ops:
  0.6 23.0 %shard_map.95 = (f32[4,8,64,128]{3,2,1,0:T(8,128)S(1)}, f32[1,128]{1,0:T(1,128)S(1)}) custom-call(s32[4]{0:T(128)} %offsets_hbm.1, f32[2,4]{1,0:T(2,128)} %bitcast.2, f32[4,8,64,128]{3,2,1,0:T(8,128)} %right_hbm.1, f32[8,64,128]{2,1,0:T(8,128)} %rate_hbm.1, f32[2,8,64]{2,1,0:T(8,128)} %fields_hbm.1, f32[1,128]{1,0:T(1,128)} %bitcast.3, s32[8,64]{1,0:T(8,128)} %regions_hbm.1, ...), custom_call_target="tpu_custom_call" | custom-call | tf_op jit(solution)/shard_map/pallas_call | solution.py:469
  23.7 1.5 %shard_map.96 = (f32[4,8,64,128]{3,2,1,0:T(8,128)}, f32[2,4]{1,0:T(2,128)}) custom-call(f32[4,8,64,128]{3,2,1,0:T(8,128)S(1)} %get-tuple-element.4.state, f32[1,128]{1,0:T(1,128)S(1)} %get-tuple-element.5.sums_ref), custom_call_target="tpu_custom_call" | custom-call | tf_op jit(solution)/shard_map/pallas_call | solution.py:531

commit v2 on v1

--- a/solution.py
+++ b/solution.py
@@ -99,7 +99,7 @@
                 (regions_hbm, regions_ref),
                 (contacts_hbm, contacts_ref),
                 (rate_hbm, rate),
-                (right_hbm, right),
+                *((right_hbm.at[c], right.at[c]) for c in range(COEFS)),
             )
         )
     ]
@@ -137,7 +137,7 @@
         for k in range(SWEEPS):
             from_high[k] = jnp.zeros(from_high.shape[1:], jnp.float32)
 
-    for load in loads[:-2]:
+    for load in loads[:6]:
         load.wait()
 
     region = regions_ref[...]
@@ -161,7 +161,7 @@
         for x in range(nx):
             target[x] = jnp.broadcast_to(turned[:, x : x + 1], (ny, width))
 
-    for load in loads[-2:]:
+    for load in loads[6:]:
         load.wait()
 
     def solve(r, px, py, diag, inv_d, inv_t):
@@ -173,7 +173,14 @@
             r[3] * inv_d,
         )
 
-    def first_state(x, carry):
+    half = nx // 2
+
+    def plane_at(i):
+        turned, step = i % 2, i // 2
+        return step + turned * (nx - 1 - 2 * step)
+
+    def first_state(i, carry):
+        x = plane_at(i)
         for y in range(0, ny, ROWS):
             rows = pl.ds(y, ROWS)
             diag = rate[x, rows] + 4.0 * diffusion
@@ -189,11 +196,14 @@
                 field[0, c, x + 1, pl.ds(PAD + y, ROWS)] = jnp.where(pinned, r[c], u[c])
         return carry
 
-    lax.fori_loop(0, nx, first_state, 0)
+    lax.fori_loop(0, half, first_state, 0)
     pl.semaphore_wait(barrier, n_energy + n_space - 2)
 
     unit_lane = lax.broadcasted_iota(jnp.int32, (8, width), 1)
-    units = [(x, y) for x in range(nx) for y in range(0, ny, 8)]
+    units = [
+        [(plane_at(i), y) for i in part for y in range(0, ny, 8)]
+        for part in (range(half), range(half, nx))
+    ]
     inner = pl.ds(PAD, ny)
 
     def to_right(k):
@@ -216,22 +226,22 @@
             device_id_type=MESH,
         )
 
-    def to_upper(k):
+    def to_upper(k, g):
         return pltpu.make_async_remote_copy(
-            src_ref=pack_high.at[k],
-            dst_ref=from_low.at[k],
-            send_sem=e_send.at[k, 0],
-            recv_sem=e_recv.at[k, 0],
+            src_ref=pack_high.at[k, g],
+            dst_ref=from_low.at[k, g],
+            send_sem=e_send.at[k, g, 0],
+            recv_sem=e_recv.at[k, g, 0],
             device_id=(e + 1, s),
             device_id_type=MESH,
         )
 
-    def to_lower(k):
+    def to_lower(k, g):
         return pltpu.make_async_remote_copy(
-            src_ref=pack_low.at[k],
-            dst_ref=from_high.at[k],
-            send_sem=e_send.at[k, 1],
-            recv_sem=e_recv.at[k, 1],
+            src_ref=pack_low.at[k, g],
+            dst_ref=from_high.at[k, g],
+            send_sem=e_send.at[k, g, 1],
+            recv_sem=e_recv.at[k, g, 1],
             device_id=(e - 1, s),
             device_id_type=MESH,
         )
@@ -243,58 +253,66 @@
         by = by % width
         return pltpu.roll(value, by, 1) if by else value
 
-    def exchange(k):
-        @pl.when(has_right)
-        def _():
-            to_right(k).start()
-
-        @pl.when(has_left)
-        def _():
-            to_left(k).start()
-
-        for q in range(pack_low.shape[1]):
+    def exchange(k, g):
+        if g == 0:
+
+            @pl.when(has_right)
+            def _():
+                to_right(k).start()
+
+            @pl.when(has_left)
+            def _():
+                to_left(k).start()
+
+        for q in range(pack_low.shape[2]):
             low = jnp.zeros((8, width), jnp.float32)
             high = jnp.zeros((8, width), jnp.float32)
-            for j, (x, y) in enumerate(units[q * groups : (q + 1) * groups]):
+            for j, (x, y) in enumerate(units[g][q * groups : (q + 1) * groups]):
                 part = field[k, 0, x + 1, pl.ds(PAD + y, 8)]
                 here = (unit_lane >= HOP * j) & (unit_lane < HOP * (j + 1))
                 low = jnp.where(here, turn(part, HOP * j), low)
                 high = jnp.where(here, turn(part, HOP * (j + 1)), high)
-            pack_low[k, q] = low
-            pack_high[k, q] = high
+            pack_low[k, g, q] = low
+            pack_high[k, g, q] = high
 
         @pl.when(has_upper)
         def _():
-            to_upper(k).start()
+            to_upper(k, g).start()
 
         @pl.when(has_lower)
         def _():
-            to_lower(k).start()
-
-    def arrive(k):
+            to_lower(k, g).start()
+
+    def arrive(k, g):
         @pl.when(has_lower)
         def _():
-            to_upper(k).wait_recv()
+            to_upper(k, g).wait_recv()
 
         @pl.when(has_upper)
         def _():
-            to_lower(k).wait_recv()
-
-        @pl.when(has_left)
-        def _():
-            to_right(k).wait_recv()
-
-        @pl.when(has_right)
-        def _():
-            to_left(k).wait_recv()
-
-        for i, (x, y) in enumerate(units):
+            to_lower(k, g).wait_recv()
+
+        for i, (x, y) in enumerate(units[g]):
             q, j = i // groups, i % groups
             beyond[x, pl.ds(y, 8)] = jnp.where(
                 unit_lane < width // 2,
-                turn(from_high[k, q], -HOP * j),
-                turn(from_low[k, q], -HOP * (j + 1)),
+                turn(from_high[k, g, q], -HOP * j),
+                turn(from_low[k, g, q], -HOP * (j + 1)),
             )
+
+        if g == 0:
+
+            @pl.when(has_left)
+            def _():
+                to_right(k).wait_recv()
+
+            @pl.when(has_right)
+            def _():
+                to_left(k).wait_recv()
+
+    exchange(0, 0)
+    lax.fori_loop(half, nx, first_state, 0)
+    exchange(0, 1)
 
     lane = lax.broadcasted_iota(jnp.int32, (ROWS, width), 1)
     velocity = jnp.broadcast_to(0.5 * speed_ref[...], (ROWS, width))
@@ -314,13 +332,13 @@
         off = cell_off[x, rows]
         below = jnp.take_along_axis(
             jnp.where(lane < width - off, f[0], outside),
-            lax.rem(lane - off + width, width),
+            jnp.where(lane < off, lane - off + width, lane - off),
             axis=1,
             mode="promise_in_bounds",
         )
         above = jnp.take_along_axis(
             jnp.where(lane < off, outside, f[0]),
-            lax.rem(lane + off, width),
+            jnp.where(lane < width - off, lane + off, lane + off - width),
             axis=1,
             mode="promise_in_bounds",
         )
@@ -349,8 +367,11 @@
             out = out + square[i : i + 8]
         return out
 
-    def sweep(k, last):
-        def plane(x, carry):
+    def sweep(k, g, start):
+        last = k == SWEEPS - 1
+
+        def plane(i, carry):
+            x = plane_at(i)
             acc = list(carry)
             for y in range(0, ny, ROWS):
                 f, resid, pinned, px, py, diag = residual(k, x, y)
@@ -365,19 +386,22 @@
                         )
             return tuple(acc)
 
-        start = tuple(jnp.zeros((8, width), jnp.float32) for _ in range(COEFS))
-        return lax.fori_loop(0, nx, plane, start)
+        return lax.fori_loop(g * half, half if g == 0 else nx, plane, start)
 
     partial = []
     store = pltpu.make_async_copy(
         field.at[SWEEPS - 1, :, pl.ds(1, nx), inner], state_ref, out_sem
     )
     for k in range(SWEEPS):
-        exchange(k)
         if k == SWEEPS - 1:
             store.start()
-        arrive(k)
-        partial.extend(sweep(k, k == SWEEPS - 1))
+        acc = tuple(jnp.zeros((8, width), jnp.float32) for _ in range(COEFS))
+        for g in range(2):
+            arrive(k, g)
+            acc = sweep(k, g, acc)
+            if k < SWEEPS - 1:
+                exchange(k + 1, g)
+        partial.extend(acc)
 
     spot = lax.broadcasted_iota(jnp.int32, (1, width), 1)
     mine = jnp.zeros((1, width), jnp.float32)
@@ -426,13 +450,15 @@
         def _():
             to_left(k).wait_send()
 
-        @pl.when(has_upper)
-        def _():
-            to_upper(k).wait_send()
-
-        @pl.when(has_lower)
-        def _():
-            to_lower(k).wait_send()
+        for g in range(2):
+
+            @pl.when(has_upper)
+            def _():
+                to_upper(k, g).wait_send()
+
+            @pl.when(has_lower)
+            def _():
+                to_lower(k, g).wait_send()
 
     for step in range(1, n_energy):
         tell(*first, step).wait_send()
@@ -445,14 +471,18 @@
 
 
 def finish(state, sums_ref, state_hbm, norms_ref, sem):
-    store = pltpu.make_async_copy(state, state_hbm, sem)
-    store.start()
+    stores = [
+        pltpu.make_async_copy(state.at[c], state_hbm.at[c], sem.at[c]) for c in range(COEFS)
+    ]
+    for store in stores:
+        store.start()
     width = sums_ref.shape[1]
     norm = jnp.broadcast_to(jnp.sqrt(sums_ref[...]), (8, width))
     for k in range(SWEEPS):
         turned = pltpu.roll(norm, width - COEFS * k, 1) if k else norm
         norms_ref[k : k + 1, :] = turned[0:1, 0:COEFS]
-    store.wait()
+    for store in stores:
+        store.wait()
 
 
 def solution(mesh):
@@ -460,12 +490,12 @@
 
     def local(right_side, rate, fields, speed, regions, contacts, offsets, phonon):
         coefs, nx, ny, width = right_side.shape
-        packs = -(-(nx * ny // 8) // (width // HOP))
+        packs = -(-((nx - nx // 2) * ny // 8) // (width // HOP))
         plane = (nx, ny, width)
         vmem = pl.BlockSpec(memory_space=pltpu.VMEM)
         hbm = pl.BlockSpec(memory_space=pl.ANY)
         f32 = jnp.float32
-        pack = pltpu.VMEM((SWEEPS, packs, 8, width), f32)
+        pack = pltpu.VMEM((SWEEPS, 2, packs, 8, width), f32)
         state, sums = pl.pallas_call(
             functools.partial(kernel, n_energy, n_space),
             out_shape=(
@@ -499,12 +529,12 @@
                 pltpu.VMEM(plane, f32),
                 pltpu.VMEM((n_energy, 1, width), f32),
                 pltpu.VMEM((n_space, 1, width), f32),
-                pltpu.SemaphoreType.DMA((8,)),
+                pltpu.SemaphoreType.DMA((7 + coefs,)),
                 pltpu.SemaphoreType.DMA,
                 pltpu.SemaphoreType.DMA((SWEEPS, 2)),
                 pltpu.SemaphoreType.DMA((SWEEPS, 2)),
-                pltpu.SemaphoreType.DMA((SWEEPS, 2)),
-                pltpu.SemaphoreType.DMA((SWEEPS, 2)),
+                pltpu.SemaphoreType.DMA((SWEEPS, 2, 2)),
+                pltpu.SemaphoreType.DMA((SWEEPS, 2, 2)),
                 pltpu.SemaphoreType.DMA((n_energy,)),
                 pltpu.SemaphoreType.DMA((n_energy,)),
                 pltpu.SemaphoreType.DMA((n_space,)),
@@ -536,7 +566,7 @@
             ),
             in_specs=[vmem, vmem],
             out_specs=(hbm, vmem),
-            scratch_shapes=[pltpu.SemaphoreType.DMA],
+            scratch_shapes=[pltpu.SemaphoreType.DMA((coefs,))],
             compiler_params=pltpu.CompilerParams(vmem_limit_bytes=8 << 20),
         )(state, sums)
 

time: 25.4 us -> 24.2 us (0.953)
  Pallas kernels: 24.6 us -> 23.4 us
    pallas_call x1, Pallas kernels: 23 us -> 21.8 us  [local(): pl.pallas_call(functools.partial(kernel, n_energy, n_space), out_shape=(p...]
where the time goes in v2:
time: 24.2 us; the launch traced here: 24 us
  Pallas kernels  23.4 us (97%)
  between operations  0.64 us (3%)
    pallas_call x1, Pallas kernels, local(): pl.pallas_call(functools.partial(kernel, n_energy, n_space), out_shape=(p...  21.8 us
    pallas_call x1, Pallas kernels, local(): pl.pallas_call(finish, out_shape=(jax.ShapeDtypeStruct(right_side.shape,...  1.56 us

profile of v2, /device:TPU:0, one launch (start us, length us, event | category | flops | bytes accessed | tf_op | source)
XLA Modules:
  0.0 24.0 jit_solution(5342176388545285429)
XLA Ops:
  0.6 21.8 %shard_map.95 = (f32[4,8,64,128]{3,2,1,0:T(8,128)S(1)}, f32[1,128]{1,0:T(1,128)S(1)}) custom-call(s32[4]{0:T(128)} %offsets_hbm.1, f32[2,4]{1,0:T(2,128)} %bitcast.2, f32[4,8,64,128]{3,2,1,0:T(8,128)} %right_hbm.1, f32[8,64,128]{2,1,0:T(8,128)} %rate_hbm.1, f32[2,8,64]{2,1,0:T(8,128)} %fields_hbm.1, f32[1,128]{1,0:T(1,128)} %bitcast.3, s32[8,64]{1,0:T(8,128)} %regions_hbm.1, ...), custom_call_target="tpu_custom_call" | custom-call | tf_op jit(solution)/shard_map/pallas_call | solution.py:499
  22.5 1.6 %shard_map.96 = (f32[4,8,64,128]{3,2,1,0:T(8,128)}, f32[2,4]{1,0:T(2,128)}) custom-call(f32[4,8,64,128]{3,2,1,0:T(8,128)S(1)} %get-tuple-element.4.state, f32[1,128]{1,0:T(1,128)S(1)} %get-tuple-element.5.sums_ref), custom_call_target="tpu_custom_call" | custom-call | tf_op jit(solution)/shard_map/pallas_call | solution.py:561

commit v3 on v2

--- a/solution.py
+++ b/solution.py
@@ -54,8 +54,7 @@
     from_low,
     from_high,
     beyond,
-    along_energy,
-    along_space,
+    sums,
     in_sem,
     out_sem,
     x_send,
@@ -64,13 +63,13 @@
     e_recv,
     n_send,
     n_recv,
-    m_send,
-    m_recv,
+    known,
 ):
     nx, ny, width = right.shape[1:]
     groups = width // HOP
     e = lax.axis_index("energy")
     s = lax.axis_index("space")
+    me = e * n_space + s
 
     barrier = pltpu.get_barrier_semaphore()
     for step in range(1, n_energy):
@@ -149,17 +148,14 @@
         off = jnp.where(inside, offsets_ref[r], off)
         absorb = jnp.where(inside, phonon_ref[0, r], absorb)
         emit = jnp.where(inside, phonon_ref[1, r], emit)
-    for source, target in (
-        (fields_ref[0], cell_x),
-        (fields_ref[1], cell_y),
-        (contacts_ref[...], cell_pin),
-        (off, cell_off),
-        (absorb, cell_absorb),
-        (emit, cell_emit),
-    ):
-        turned = source.T
-        for x in range(nx):
-            target[x] = jnp.broadcast_to(turned[:, x : x + 1], (ny, width))
+
+    def spread(*pairs):
+        for source, target in pairs:
+            turned = source.T
+            for x in range(nx):
+                target[x] = jnp.broadcast_to(turned[:, x : x + 1], (ny, width))
+
+    spread((fields_ref[0], cell_x), (fields_ref[1], cell_y), (contacts_ref[...], cell_pin))
 
     for load in loads[6:]:
         load.wait()
@@ -198,6 +194,13 @@
 
     lax.fori_loop(0, half, first_state, 0)
     pl.semaphore_wait(barrier, n_energy + n_space - 2)
+    for step in range(1, n_energy):
+        pl.semaphore_signal(
+            known,
+            inc=1,
+            device_id=(lax.rem(e + step, n_energy), s),
+            device_id_type=MESH,
+        )
 
     unit_lane = lax.broadcasted_iota(jnp.int32, (8, width), 1)
     units = [
@@ -313,6 +316,7 @@
     exchange(0, 0)
     lax.fori_loop(half, nx, first_state, 0)
     exchange(0, 1)
+    spread((off, cell_off), (absorb, cell_absorb), (emit, cell_emit))
 
     lane = lax.broadcasted_iota(jnp.int32, (ROWS, width), 1)
     velocity = jnp.broadcast_to(0.5 * speed_ref[...], (ROWS, width))
@@ -408,38 +412,24 @@
     for i, value in enumerate(partial):
         whole = jnp.sum(jnp.sum(value, axis=0, keepdims=True), axis=1, keepdims=True)
         mine = jnp.where(spot == i, whole, mine)
-    along_energy[e] = mine
-
-    def tell(sums, size, place, to, sems, step):
+    sums[me] = mine
+    pl.semaphore_wait(known, n_energy - 1)
+
+    def tell(de, ds, rows):
         return pltpu.make_async_remote_copy(
-            src_ref=sums.at[place],
-            dst_ref=sums.at[place],
-            send_sem=sems[0].at[step],
-            recv_sem=sems[1].at[place],
-            device_id=to(lax.rem(place + step, size)),
-            device_id_type=MESH,
-        )
-
-    def heard(sums, size, place, to, sems, step):
-        other = lax.rem(place + step, size)
-        return pltpu.make_async_remote_copy(
-            src_ref=sums.at[other],
-            dst_ref=sums.at[other],
-            send_sem=sems[0].at[step],
-            recv_sem=sems[1].at[other],
-            device_id=to(other),
-            device_id_type=MESH,
-        )
-
-    first = (along_energy, n_energy, e, lambda i: (i, s), (n_send, n_recv))
-    second = (along_space, n_space, s, lambda i: (e, i), (m_send, m_recv))
-    for step in range(1, n_energy):
-        tell(*first, step).start()
-    for step in range(1, n_energy):
-        heard(*first, step).wait_recv()
-    along_space[s] = jnp.sum(along_energy[...], axis=0)
-    for step in range(1, n_space):
-        tell(*second, step).start()
+            src_ref=sums.at[rows],
+            dst_ref=sums.at[rows],
+            send_sem=n_send,
+            recv_sem=n_recv,
+            device_id=(lax.rem(e + de, n_energy), lax.rem(s + ds, n_space)),
+            device_id_type=MESH,
+        )
+
+    own = pl.ds(me, 1)
+    for ds in sorted(range(n_space), key=lambda d: -min(d, n_space - d)):
+        for de in range(n_energy):
+            if (de, ds) != (0, 0):
+                tell(de, ds, own).start()
     for k in range(SWEEPS):
 
         @pl.when(has_right)
@@ -460,14 +450,11 @@
             def _():
                 to_lower(k, g).wait_send()
 
-    for step in range(1, n_energy):
-        tell(*first, step).wait_send()
     store.wait()
-    for step in range(1, n_space):
-        heard(*second, step).wait_recv()
-    for step in range(1, n_space):
-        tell(*second, step).wait_send()
-    sums_ref[...] = jnp.sum(along_space[...], axis=0)
+    others = tell(0, 1, pl.ds(0, n_energy * n_space - 1))
+    others.wait_recv()
+    others.wait_send()
+    sums_ref[...] = jnp.sum(sums[...], axis=0)
 
 
 def finish(state, sums_ref, state_hbm, norms_ref, sem):
@@ -527,18 +514,16 @@
                 pack,
                 pack,
                 pltpu.VMEM(plane, f32),
-                pltpu.VMEM((n_energy, 1, width), f32),
-                pltpu.VMEM((n_space, 1, width), f32),
+                pltpu.VMEM((n_energy * n_space, 1, width), f32),
                 pltpu.SemaphoreType.DMA((7 + coefs,)),
                 pltpu.SemaphoreType.DMA,
                 pltpu.SemaphoreType.DMA((SWEEPS, 2)),
                 pltpu.SemaphoreType.DMA((SWEEPS, 2)),
                 pltpu.SemaphoreType.DMA((SWEEPS, 2, 2)),
                 pltpu.SemaphoreType.DMA((SWEEPS, 2, 2)),
-                pltpu.SemaphoreType.DMA((n_energy,)),
-                pltpu.SemaphoreType.DMA((n_energy,)),
-                pltpu.SemaphoreType.DMA((n_space,)),
-                pltpu.SemaphoreType.DMA((n_space,)),
+                pltpu.SemaphoreType.DMA,
+                pltpu.SemaphoreType.DMA,
+                pltpu.SemaphoreType.REGULAR,
             ],
             compiler_params=pltpu.CompilerParams(
                 collective_id=0, has_side_effects=True, vmem_limit_bytes=24 << 20

time: 24.2 us -> 21.9 us (0.905)
  Pallas kernels: 23.4 us -> 21.1 us
    pallas_call x1, Pallas kernels: 21.8 us -> 19.6 us  [local(): pl.pallas_call(functools.partial(kernel, n_energy, n_space), out_shape=(p...]
where the time goes in v3:
time: 21.9 us; the launch traced here: 21.8 us
  Pallas kernels  21.1 us (96%)
  between operations  0.64 us (3%)
    pallas_call x1, Pallas kernels, local(): pl.pallas_call(functools.partial(kernel, n_energy, n_space), out_shape=(p...  19.6 us
    pallas_call x1, Pallas kernels, local(): pl.pallas_call(finish, out_shape=(jax.ShapeDtypeStruct(right_side.shape,...  1.56 us

profile of v3, /device:TPU:0, one launch (start us, length us, event | category | flops | bytes accessed | tf_op | source)
XLA Modules:
  0.0 21.8 jit_solution(6697032179500286788)
XLA Ops:
  0.6 19.6 %shard_map.95 = (f32[4,8,64,128]{3,2,1,0:T(8,128)S(1)}, f32[1,128]{1,0:T(1,128)S(1)}) custom-call(s32[4]{0:T(128)} %offsets_hbm.1, f32[2,4]{1,0:T(2,128)} %bitcast.2, f32[4,8,64,128]{3,2,1,0:T(8,128)} %right_hbm.1, f32[8,64,128]{2,1,0:T(8,128)} %rate_hbm.1, f32[2,8,64]{2,1,0:T(8,128)} %fields_hbm.1, f32[1,128]{1,0:T(1,128)} %bitcast.3, s32[8,64]{1,0:T(8,128)} %regions_hbm.1, ...), custom_call_target="tpu_custom_call" | custom-call | tf_op jit(solution)/shard_map/pallas_call | solution.py:486
  20.2 1.6 %shard_map.96 = (f32[4,8,64,128]{3,2,1,0:T(8,128)}, f32[2,4]{1,0:T(2,128)}) custom-call(f32[4,8,64,128]{3,2,1,0:T(8,128)S(1)} %get-tuple-element.4.state, f32[1,128]{1,0:T(1,128)S(1)} %get-tuple-element.5.sums_ref), custom_call_target="tpu_custom_call" | custom-call | tf_op jit(solution)/shard_map/pallas_call | solution.py:546
